TPU v7x, 256 devices: a whole 4x4x8 slice. The times are simulated.
256 devices in a mesh: site: 4 (over x), fsdp: 64 (over z, y, core).
Axes of the slice: x: 4, y: 4, z: 8, core: 2. Of those that a mesh axis runs over, the one named last changes fastest.
Arguments:
- held_input: bfloat16 [4, 32768, 1536], P('site', 'fsdp'), may hold values from -16 to 16
- held_cotangent: bfloat16 [4, 32768, 1536], P('site', 'fsdp'), may hold values from -6 to 6
- proj_weight: bfloat16 [1536, 1536], P('fsdp'), may hold values from -0.15625 to 0.15625
- stem_weight: bfloat16 [3, 512, 1536], P(None, 'fsdp'), may hold values from -0.15625 to 0.15625
- seg_counts: int32 [4, 64], P('site'), may hold values from 1 to 128, 4096 in all within a row
Outputs:
- stem_grad: bfloat16 [4, 131072, 512], P('site', 'fsdp')
- weight_grad: float32 [1536, 1536], P('fsdp')
Inputs may be any that keep to these rules, and one draw needn't show every extreme that they name: `seg_counts`: in every group the 64 counts sum to 4096, so that every holder slot is used; one owner has exactly 128, and a holder keeps at most 2 segments of one owner, a bound reached in every draw.
All inputs are finite; a program needn't handle non-finite values.
Results may differ from a plain program's by a relative error of at most 0.0049.
Values may be sent and summed in bfloat16 or wider, within the bound.
A program may use at most 128 MiB of HBM per device.

v0:
```python
import math
import jax
import jax.numpy as jnp
from jax import lax
from jax.sharding import PartitionSpec as P

D = 1536
SEG = 8
HOLD = 64
OWN_SEG = 128
EPSILON = 1e-05


def stem_taps(frames, stem_weight):
    return jnp.einsum(
        "rd,kcd->krc",
        frames,
        lax.all_gather(stem_weight, "fsdp", axis=1, tiled=True),
        preferred_element_type=jnp.float32,
    )


def body(held_input, held_cotangent, proj_weight, stem_weight, seg_counts):
    group_size = lax.axis_size("fsdp")
    capacity = 2 * ((OWN_SEG + 2 * group_size - 1) // (2 * group_size))
    my_index = lax.axis_index("fsdp")
    inputs = held_input[0].astype(jnp.float32)
    cotangent = held_cotangent[0]
    row_mean = jnp.mean(inputs, axis=-1, keepdims=True)
    centered = inputs - row_mean
    variance = jnp.mean(centered * centered, axis=-1, keepdims=True)
    inverse = lax.rsqrt(variance + EPSILON)
    normed = centered * inverse
    normed_bf = normed.astype(jnp.bfloat16)
    proj_back = lax.dot_general(
        cotangent,
        lax.all_gather(proj_weight, "fsdp", axis=0, tiled=True),
        (((1,), (1,)), ((), ())),
        preferred_element_type=jnp.float32,
    )
    input_grad = cotangent.astype(jnp.float32) + inverse * (
        proj_back
        - jnp.mean(proj_back, axis=-1, keepdims=True)
        - normed * jnp.mean(proj_back * normed, axis=-1, keepdims=True)
    )
    input_grad = input_grad.astype(jnp.bfloat16)
    counts = seg_counts[0]
    endings = jnp.cumsum(counts)
    starts = endings - counts
    slot_ids = jnp.arange(HOLD, dtype=jnp.int32)
    item_index = 2 * (slot_ids // 2 * group_size + my_index) + slot_ids % 2
    owner_ids = jnp.sum((item_index[:, None] >= endings[None, :]).astype(jnp.int32), axis=1)
    earlier = (slot_ids[None, :] < slot_ids[:, None]) & (owner_ids[None, :] == owner_ids[:, None])
    rank_ids = jnp.sum(earlier.astype(jnp.int32), axis=1)
    target = owner_ids * capacity + rank_ids
    positions = jnp.arange(group_size * capacity, dtype=jnp.int32)
    matched = target[None, :] == positions[:, None]
    filled = jnp.any(matched, axis=1)
    source = jnp.sum(jnp.where(matched, slot_ids[None, :], 0), axis=1)
    owner_hit = jnp.arange(group_size, dtype=jnp.int32) == my_index
    my_count = jnp.sum(jnp.where(owner_hit, counts, 0))
    my_start = jnp.sum(jnp.where(owner_hit, starts, 0))
    segment = jnp.arange(OWN_SEG, dtype=jnp.int32)
    is_live = segment < my_count
    holder = (my_start + segment) // 2 % group_size
    before = (
        (segment[None, :] < segment[:, None])
        & (holder[None, :] == holder[:, None])
        & is_live[None, :]
    )
    holder_rank = jnp.sum(before.astype(jnp.int32), axis=1)
    row_index = jnp.where(is_live, holder * capacity + holder_rank, 0)
    held_segments = input_grad.reshape(HOLD, SEG, D)
    zero_bf = jnp.zeros((), jnp.bfloat16)
    send_rows = jnp.where(filled[:, None, None], jnp.take(held_segments, source, axis=0), zero_bf)
    received = lax.all_to_all(
        send_rows.reshape(group_size, capacity, SEG, D),
        "fsdp",
        split_axis=0,
        concat_axis=0,
        tiled=True,
    )
    picked = jnp.take(received.reshape(group_size * capacity, SEG, D), row_index, axis=0)
    frames = jnp.where(is_live[:, None, None], picked, zero_bf).reshape(OWN_SEG * SEG, D)
    tap_terms = stem_taps(frames, stem_weight)
    shifted = jnp.concatenate(
        [tap_terms[0][1:], jnp.zeros((1, tap_terms.shape[2]), jnp.float32)], 0
    )
    odd_rows = tap_terms[2] + shifted
    stem_rows = (
        jnp.stack([tap_terms[1], odd_rows], 1)
        .reshape(2 * OWN_SEG * SEG, tap_terms.shape[2])
        .astype(jnp.bfloat16)
    )
    shard_sum = lax.psum_scatter(
        lax.dot_general(
            normed_bf, cotangent, (((0,), (0,)), ((), ())), preferred_element_type=jnp.float32
        ),
        "fsdp",
        scatter_dimension=0,
        tiled=True,
    )
    shard_sum = lax.psum(shard_sum, "site")
    weight_grad = shard_sum / math.sqrt(lax.axis_size("site") * group_size * HOLD * SEG)
    return (stem_rows[None], weight_grad)


def solution(mesh):
    placed = (
        P("site", "fsdp", None),
        P("site", "fsdp", None),
        P("fsdp", None),
        P(None, "fsdp", None),
        P("site", None),
    )
    return jax.shard_map(
        body,
        mesh=mesh,
        in_specs=placed,
        out_specs=(P("site", "fsdp", None), P("fsdp", None)),
        check_vma=False,
    )
```

profile of v0, /device:TPU:1, one launch (start us, length us, event | category | flops | bytes accessed | tf_op | source)
XLA Modules:
  0.0 408.3 jit_solution(15506953780961973677)
XLA Ops:
  7.2 0.0 reduce-scatter.4.cloned.1.call-start
  7.2 1.8 convert_reduce_fusion
  9.1 2.0 fusion.10
  11.1 5.3 %fusion.25 = f32[1536,1536]{1,0:T(8,128)} fusion(bf16[1,512,1536]{2,1,0:T(8,128)(2,1)S(1)} %copy-done, bf16[1,512,1536]{2,1,0:T(8,128)(2,1)S(1)} %copy-done.1, f32[512]{0:T(512)S(1)} %add_rsqrt_fusion, f32[512]{0:T(512)S(1)} %broadcast_multiply_fusion.3), kind=kOutput, calls=%fused_computation.33 | convolution fusion | flops 2419064832 | bytes 12587008 | tf_op jit(solution)/shard_map/dot_general | solution.py:96
  16.4 0.0 reduce-scatter.4.cloned.1.call-update
  16.4 0.0 all-gather.3.cloned.1.call-start
  16.5 0.7 all-gather.3.cloned.1.call-update
  17.2 0.0 all-reduce.4.cloned.1.call-start
  17.2 152.7 %reduce-scatter.4.cloned.1.call-done = f32[24,1536]{1,0:T(8,128)} async-done(((f32[1536,1536]{1,0:T(8,128)}), f32[24,1536]{1,0:T(8,128)}) %reduce-scatter.4.cloned.1.call-update) | async-done | bytes 147472
  169.9 0.0 all-gather.5.cloned.1.call-start
  170.0 0.5 all-gather.5.cloned.1.call-update
  170.5 0.1 copy.12
  170.6 0.1 reduce-window.8
  170.7 0.1 reduce.1
  170.8 0.6 fusion.45
  171.5 0.2 convert_reduce_fusion.3
  171.6 0.2 convert_reduce_fusion.2
  171.8 0.1 fusion.39
  171.9 0.2 broadcast_in_dim.98
  172.1 0.1 select_reduce_fusion
  172.2 0.1 reduce_sum.102
  172.4 83.0 %all-gather.3.cloned.1.call-done = bf16[1536,1536]{1,0:T(8,128)(2,1)} async-done(((bf16[24,1536]{1,0:T(8,128)(2,1)}), bf16[1536,1536]{1,0:T(8,128)(2,1)}) %all-gather.3.cloned.1.call-update) | async-done | bytes 4718608 | tf_op jit(solution)/shard_map/all_gather | solution.py:37
  255.4 4.9 %fusion.55 = (f32[512]{0:T(512)S(1)}, f32[512]{0:T(512)S(1)}, f32[512,1536]{1,0:T(8,128)S(1)}) fusion(f32[512]{0:T(512)S(1)} %add_rsqrt_fusion, f32[512]{0:T(512)S(1)} %broadcast_multiply_fusion.3, bf16[1,512,1536]{2,1,0:T(8,128)(2,1)S(1)} %copy-done, bf16[1536,1536]{1,0:T(8,128)(2,1)} %all-gather.3.cloned.1.call-done, bf16[1,512,1536]{2,1,0:T(8,128)(2,1)S(1)} %copy-done.1), kind=kOutput, calls=%fused_computation.107 | convolution fusion | flops 2420636672 | bytes 11018240 | tf_op jit(solution)/shard_map/dot_general | solution.py:35
  260.3 1.2 fusion.27
  261.5 2.5 gather_fusion
  264.0 3.3 select_select_fusion
  267.3 6.3 %all-to-all-start = ((bf16[64,2,8,1536]{3,2,1,0:T(8,128)(2,1)}), bf16[64,2,8,1536]{3,2,1,0:T(8,128)(2,1)S(1)}, u32[]{:S(2)}, u32[]{:S(2)}) async-start(bf16[64,2,8,1536]{3,2,1,0:T(8,128)(2,1)} %select_select_fusion), calls=%async_computation | async-start | bytes 6291456 | tf_op jit(solution)/shard_map/all_to_all | solution.py:76
  273.6 0.7 iota_compare_fusion.3
  274.3 0.7 and_select_fusion.4
  274.9 0.2 convert_reduce_fusion.1
  275.1 1.3 compare_and_fusion.1
  276.4 0.1 broadcast_in_dim.95
  276.5 0.1 broadcast_in_dim.96
  276.6 0.1 broadcast_in_dim.92
  276.7 0.1 broadcast_in_dim.93
  276.8 1.3 fusion.52
  278.2 21.2 %all-reduce.4.cloned.1.call-done = f32[24,1536]{1,0:T(8,128)} async-done(((f32[24,1536]{1,0:T(8,128)}), f32[24,1536]{1,0:T(8,128)}) %all-reduce.4.cloned.1.call-update) | async-done | bytes 147472 | tf_op jit(solution)/shard_map/psum | solution.py:103
  299.4 1.6 broadcast_multiply_fusion
  300.9 48.2 %all-to-all-done = bf16[64,2,8,1536]{3,2,1,0:T(8,128)(2,1)S(1)} async-done(((bf16[64,2,8,1536]{3,2,1,0:T(8,128)(2,1)}), bf16[64,2,8,1536]{3,2,1,0:T(8,128)(2,1)S(1)}, u32[]{:S(2)}, u32[]{:S(2)}) %all-to-all-start) | async-done | bytes 3145760 | tf_op jit(solution)/shard_map/all_to_all | solution.py:76
  349.1 2.4 gather_fusion.1
  351.5 36.3 %all-gather.5.cloned.1.call-done = bf16[3,512,1536]{2,1,0:T(8,128)(2,1)} async-done(((bf16[3,8,1536]{2,1,0:T(8,128)(2,1)}), bf16[3,512,1536]{2,1,0:T(8,128)(2,1)}) %all-gather.5.cloned.1.call-update) | async-done | bytes 4718608 | tf_op jit(solution)/shard_map/all_gather | solution.py:18
  387.9 8.4 %fusion.19 = f32[3,1024,512]{2,1,0:T(8,128)S(1)} fusion(bf16[3,512,1536]{2,1,0:T(8,128)(2,1)} %all-gather.5.cloned.1.call-done, bf16[128,8,1536]{2,1,0:T(8,128)(2,1)} %gather_fusion.1, pred[1024]{0:T(1024)(128)(4,1)S(1)} %broadcast_in_dim.96, pred[1024]{0:T(1024)(128)(4,1)S(1)} %broadcast_in_dim.93), kind=kOutput, calls=%fused_computation.25 | convolution fusion | flops 4834983936 | bytes 14157824 | tf_op jit(solution)/shard_map/rd,kcd->krc/dot_general | solution.py:15
  396.2 0.1 fusion.35
  396.4 0.2 slice_bitcast_fusion
  396.6 0.6 fusion.36
  397.2 0.2 pad_maximum_fusion
  397.4 2.2 copy.13
  399.6 2.2 convert_element_type.46
  (17 shorter events, 0.1 us)
Async XLA Ops:
  7.2 3.9 copy-start
  7.2 3.9 copy-start.1
  7.2 162.7 %reduce-scatter.4.cloned.1.call-start = ((), (), s32[]{:S(2)}) async-start(), calls=%async_computation.5 | async-start | bytes 9584640
  16.4 154.1 %copy-start.3 = (s32[1,64]{1,0:T(1,128)S(1)}, s32[1,64]{1,0:T(1,128)}, u32[]{:S(2)}) copy-start(s32[1,64]{1,0:T(1,128)} %param.9) | copy-start | bytes 772
  16.4 239.0 %all-gather.3.cloned.1.call-start = ((), (), s32[]{:S(2)}) async-start(), calls=%async_computation.2 | async-start | bytes 4792320 | tf_op jit(solution)/shard_map/all_gather | solution.py:37
  17.2 282.2 %all-reduce.4.cloned.1.call-start = ((), (), s32[]{:S(2)}) async-start(), calls=%async_computation.4 | async-start | bytes 294912 | tf_op jit(solution)/shard_map/psum | solution.py:103
  169.9 217.9 %all-gather.5.cloned.1.call-start = ((), (), s32[]{:S(2)}) async-start(), calls=%async_computation.3 | async-start | bytes 4792320 | tf_op jit(solution)/shard_map/all_gather | solution.py:18
  255.4 4.9 %copy-start.2 = (bf16[1,512,1536]{2,1,0:T(8,128)(2,1)S(1)}, bf16[1,512,1536]{2,1,0:T(8,128)(2,1)}, u32[]{:S(2)}) copy-start(bf16[1,512,1536]{2,1,0:T(8,128)(2,1)} %param.6) | copy-start | bytes 4718596
  267.3 81.8 %all-to-all-start = ((bf16[64,2,8,1536]{3,2,1,0:T(8,128)(2,1)}), bf16[64,2,8,1536]{3,2,1,0:T(8,128)(2,1)S(1)}, u32[]{:S(2)}, u32[]{:S(2)}) async-start(bf16[64,2,8,1536]{3,2,1,0:T(8,128)(2,1)} %select_select_fusion), calls=%async_computation | async-start | bytes 6291456 | tf_op jit(solution)/shard_map/all_to_all | solution.py:76
Sparse Core Ops, SparseCore 0:
  16.5 153.3 reduce-scatter.3
  172.6 82.6 all-gather.2
  257.7 41.6 all-reduce.3
  302.3 85.5 all-gather.4
where the time goes:
time: 409 us; the launch traced here: 408 us
  waiting for transfers between devices  343 us (84%)
  matrix products  18.6 us (5%)
  other arithmetic  16.2 us (4%)
  between operations  14 us (3%)
  local copies, waits for them, and re-layouts  10.4 us (3%)
  starting transfers between devices  6.46 us (2%)
    unnamed x5, waiting for transfers between devices  154 us
    all_gather x1, waiting for transfers between devices, body(): lax.all_gather(proj_weight, 'fsdp', axis=0, tiled=True)  83 us
    all_to_all x1, waiting for transfers between devices, body(): lax.all_to_all(send_rows.reshape(group_size, capacity, SEG, D), 'fsdp', s...  48.2 us
    all_gather x1, waiting for transfers between devices, stem_taps(): lax.all_gather(stem_weight, 'fsdp', axis=1, tiled=True)  36.3 us
    psum x1, waiting for transfers between devices, body(): shard_sum = lax.psum(shard_sum, 'site')  21.2 us
    dot_general x1, matrix products, stem_taps(): jnp.einsum('rd,kcd->krc', frames, lax.all_gather(stem_weight, 'fsdp', axi...  8.38 us
  transfers between devices with their start and end apart: 5, of which 5 were waited for; matrix products, arithmetic and copies ran while one was open for 5% of the time, Pallas kernels for 0%

commit v1 on v0

--- a/solution.py
+++ b/solution.py
@@ -34,7 +34,12 @@
     normed_bf = normed.astype(jnp.bfloat16)
     proj_back = lax.dot_general(
         cotangent,
-        lax.all_gather(proj_weight, "fsdp", axis=0, tiled=True),
+        jnp.concatenate(
+            lax.all_to_all(
+                jnp.stack([proj_weight for _ in range(lax.axis_size("fsdp"))]), "fsdp", 0, 0
+            ),
+            0,
+        ),
         (((1,), (1,)), ((), ())),
         preferred_element_type=jnp.float32,
     )

time: 409 us -> 355 us (0.87)
  waiting for transfers between devices: 343 us -> 266 us
  starting transfers between devices: 6.46 us -> 26 us
    all_gather x1 -> x0, waiting for transfers between devices: 83 us -> none  [body(): lax.all_gather(proj_weight, 'fsdp', axis=0, tiled=True)]
    all_to_all x0 -> x1, starting transfers between devices: none -> 13.5 us  [body(): lax.all_to_all(jnp.stack([proj_weight for _ in range(lax.axis_size('fsdp'...]
    unnamed x5 -> x4, waiting for transfers between devices: 154 us -> 163 us
    all_to_all x1, starting transfers between devices: 6.3 us -> 12.4 us  [body(): lax.all_to_all(send_rows.reshape(group_size, capacity, SEG, D), 'fsdp', s...]
  transfers between devices with their start and end apart: 5 -> 5, of which waited for: 5 -> 4; matrix products, arithmetic and copies ran while one was open for 5% -> 7% of each run, Pallas kernels for 0% -> 0%
where the time goes in v1:
time: 355 us
  waiting for transfers between devices  266 us (75%)
  starting transfers between devices  26 us (7%)
  matrix products  18.6 us (5%)
  other arithmetic  16.2 us (5%)
  between operations  14 us (4%)
  local copies, waits for them, and re-layouts  13.7 us (4%)
    unnamed x4, waiting for transfers between devices  163 us
    all_to_all x1, waiting for transfers between devices, body(): lax.all_to_all(send_rows.reshape(group_size, capacity, SEG, D), 'fsdp', s...  50.7 us
    all_gather x1, waiting for transfers between devices, stem_taps(): lax.all_gather(stem_weight, 'fsdp', axis=1, tiled=True)  33.8 us
    psum x1, waiting for transfers between devices, body(): shard_sum = lax.psum(shard_sum, 'site')  18.3 us
    all_to_all x1, starting transfers between devices, body(): lax.all_to_all(jnp.stack([proj_weight for _ in range(lax.axis_size('fsdp'...  13.5 us
    all_to_all x1, starting transfers between devices, body(): lax.all_to_all(send_rows.reshape(group_size, capacity, SEG, D), 'fsdp', s...  12.4 us
    dot_general x1, matrix products, stem_taps(): jnp.einsum('rd,kcd->krc', frames, lax.all_gather(stem_weight, 'fsdp', axi...  8.38 us
  transfers between devices with their start and end apart: 5, of which 4 were waited for; matrix products, arithmetic and copies ran while one was open for 7% of the time, Pallas kernels for 0%

profile of v1, /device:TPU:1, one launch (start us, length us, event | category | flops | bytes accessed | tf_op | source)
XLA Modules:
  0.0 354.7 jit_solution(15372905510068725123)
XLA Ops:
  7.2 0.0 reduce-scatter.4.cloned.1.call-start
  7.2 1.8 convert_reduce_fusion
  9.1 2.0 fusion.10
  11.1 5.3 %fusion.25 = f32[1536,1536]{1,0:T(8,128)} fusion(bf16[1,512,1536]{2,1,0:T(8,128)(2,1)S(1)} %copy-done, bf16[1,512,1536]{2,1,0:T(8,128)(2,1)S(1)} %copy-done.1, f32[512]{0:T(512)S(1)} %add_rsqrt_fusion, f32[512]{0:T(512)S(1)} %broadcast_multiply_fusion.3), kind=kOutput, calls=%fused_computation.33 | convolution fusion | flops 2419064832 | bytes 12587008 | tf_op jit(solution)/shard_map/dot_general | solution.py:101
  16.4 0.0 reduce-scatter.4.cloned.1.call-update
  16.4 0.9 copy-done.3
  17.3 2.4 stack.8
  19.7 13.5 %all-to-all-start = ((bf16[64,24,1536]{2,1,0:T(8,128)(2,1)}), bf16[64,24,1536]{2,1,0:T(8,128)(2,1)}, u32[]{:S(2)}, u32[]{:S(2)}) async-start(bf16[64,24,1536]{2,1,0:T(8,128)(2,1)} %stack.8), calls=%async_computation | async-start | bytes 9437184 | tf_op jit(solution)/shard_map/all_to_all | solution.py:38
  33.2 0.0 all-reduce.4.cloned.1.call-start
  33.2 162.6 %reduce-scatter.4.cloned.1.call-done = f32[24,1536]{1,0:T(8,128)} async-done(((f32[1536,1536]{1,0:T(8,128)}), f32[24,1536]{1,0:T(8,128)}) %reduce-scatter.4.cloned.1.call-update) | async-done | bytes 147472
  195.9 0.0 all-gather.2.cloned.1.call-start
  195.9 0.7 all-gather.2.cloned.1.call-update
  196.6 0.1 copy.12
  196.7 0.1 reduce-window.8
  196.8 0.1 reduce.1
  196.9 0.6 fusion.45
  197.6 0.2 convert_reduce_fusion.3
  197.7 0.2 convert_reduce_fusion.2
  197.9 0.1 select_reduce_fusion
  198.0 0.1 reduce_sum.102
  198.2 0.1 fusion.39
  198.3 0.2 broadcast_in_dim.98
  198.5 4.9 %fusion.55 = (f32[512]{0:T(512)S(1)}, f32[512]{0:T(512)S(1)}, f32[512,1536]{1,0:T(8,128)S(1)}) fusion(f32[512]{0:T(512)S(1)} %add_rsqrt_fusion, f32[512]{0:T(512)S(1)} %broadcast_multiply_fusion.3, bf16[1,512,1536]{2,1,0:T(8,128)(2,1)S(1)} %copy-done, bf16[1536,1536]{1,0:T(8,128)(2,1)} %bitcast.4, bf16[1,512,1536]{2,1,0:T(8,128)(2,1)S(1)} %copy-done.1), kind=kOutput, calls=%fused_computation.107 | convolution fusion | flops 2420636672 | bytes 11018240 | tf_op jit(solution)/shard_map/dot_general | solution.py:35
  203.4 1.2 fusion.27
  204.6 2.5 gather_fusion
  207.1 3.3 select_select_fusion
  210.4 12.4 %all-to-all-start.1 = ((bf16[64,2,8,1536]{3,2,1,0:T(8,128)(2,1)}), bf16[64,2,8,1536]{3,2,1,0:T(8,128)(2,1)S(1)}, u32[]{:S(2)}, u32[]{:S(2)}) async-start(bf16[64,2,8,1536]{3,2,1,0:T(8,128)(2,1)} %select_select_fusion), calls=%async_computation.1 | async-start | bytes 6291456 | tf_op jit(solution)/shard_map/all_to_all | solution.py:81
  222.8 0.7 iota_compare_fusion.3
  223.5 0.7 and_select_fusion.4
  224.2 0.2 convert_reduce_fusion.1
  224.3 1.3 compare_and_fusion.1
  225.7 0.1 broadcast_in_dim.95
  225.8 0.1 broadcast_in_dim.96
  225.9 0.1 broadcast_in_dim.92
  225.9 0.1 broadcast_in_dim.93
  226.0 1.3 fusion.52
  227.4 18.3 %all-reduce.4.cloned.1.call-done = f32[24,1536]{1,0:T(8,128)} async-done(((f32[24,1536]{1,0:T(8,128)}), f32[24,1536]{1,0:T(8,128)}) %all-reduce.4.cloned.1.call-update) | async-done | bytes 147472 | tf_op jit(solution)/shard_map/psum | solution.py:108
  245.7 1.6 broadcast_multiply_fusion
  247.3 50.7 %all-to-all-done.1 = bf16[64,2,8,1536]{3,2,1,0:T(8,128)(2,1)S(1)} async-done(((bf16[64,2,8,1536]{3,2,1,0:T(8,128)(2,1)}), bf16[64,2,8,1536]{3,2,1,0:T(8,128)(2,1)S(1)}, u32[]{:S(2)}, u32[]{:S(2)}) %all-to-all-start.1) | async-done | bytes 3145760 | tf_op jit(solution)/shard_map/all_to_all | solution.py:81
  298.0 2.4 gather_fusion.1
  300.4 33.8 %all-gather.2.cloned.1.call-done = bf16[3,512,1536]{2,1,0:T(8,128)(2,1)} async-done(((bf16[3,8,1536]{2,1,0:T(8,128)(2,1)}), bf16[3,512,1536]{2,1,0:T(8,128)(2,1)}) %all-gather.2.cloned.1.call-update) | async-done | bytes 4718608 | tf_op jit(solution)/shard_map/all_gather | solution.py:18
  334.3 8.4 %fusion.19 = f32[3,1024,512]{2,1,0:T(8,128)S(1)} fusion(bf16[3,512,1536]{2,1,0:T(8,128)(2,1)} %all-gather.2.cloned.1.call-done, bf16[128,8,1536]{2,1,0:T(8,128)(2,1)} %gather_fusion.1, pred[1024]{0:T(1024)(128)(4,1)S(1)} %broadcast_in_dim.96, pred[1024]{0:T(1024)(128)(4,1)S(1)} %broadcast_in_dim.93), kind=kOutput, calls=%fused_computation.25 | convolution fusion | flops 4834983936 | bytes 14157824 | tf_op jit(solution)/shard_map/rd,kcd->krc/dot_general | solution.py:15
  342.6 0.2 slice_bitcast_fusion
  342.9 0.1 fusion.35
  343.0 0.6 fusion.36
  343.6 0.2 pad_maximum_fusion
  343.8 2.2 copy.13
  346.0 2.2 convert_element_type.46
  (19 shorter events, 0.1 us)
Async XLA Ops:
  7.2 3.9 %copy-start = (bf16[1,512,1536]{2,1,0:T(8,128)(2,1)S(1)}, bf16[1,512,1536]{2,1,0:T(8,128)(2,1)}, u32[]{:S(2)}) copy-start(bf16[1,512,1536]{2,1,0:T(8,128)(2,1)} %param.5) | copy-start | bytes 4718596
  7.2 3.9 %copy-start.1 = (bf16[1,512,1536]{2,1,0:T(8,128)(2,1)S(1)}, bf16[1,512,1536]{2,1,0:T(8,128)(2,1)}, u32[]{:S(2)}) copy-start(bf16[1,512,1536]{2,1,0:T(8,128)(2,1)} %param.6) | copy-start | bytes 4718596
  7.2 188.6 %reduce-scatter.4.cloned.1.call-start = ((), (), s32[]{:S(2)}) async-start(), calls=%async_computation.5 | async-start | bytes 9584640
  16.4 0.9 copy-start.3
  19.7 176.9 %copy-start.4 = (s32[1,64]{1,0:T(1,128)S(1)}, s32[1,64]{1,0:T(1,128)}, u32[]{:S(2)}) copy-start(s32[1,64]{1,0:T(1,128)} %param.9) | copy-start | bytes 772
  19.7 178.8 %all-to-all-start = ((bf16[64,24,1536]{2,1,0:T(8,128)(2,1)}), bf16[64,24,1536]{2,1,0:T(8,128)(2,1)}, u32[]{:S(2)}, u32[]{:S(2)}) async-start(bf16[64,24,1536]{2,1,0:T(8,128)(2,1)} %stack.8), calls=%async_computation | async-start | bytes 9437184 | tf_op jit(solution)/shard_map/all_to_all | solution.py:38
  33.2 212.6 %all-reduce.4.cloned.1.call-start = ((), (), s32[]{:S(2)}) async-start(), calls=%async_computation.4 | async-start | bytes 294912 | tf_op jit(solution)/shard_map/psum | solution.py:108
  195.9 138.4 %all-gather.2.cloned.1.call-start = ((), (), s32[]{:S(2)}) async-start(), calls=%async_computation.3 | async-start | bytes 4792320 | tf_op jit(solution)/shard_map/all_gather | solution.py:18
  198.5 4.9 %copy-start.2 = (bf16[1,512,1536]{2,1,0:T(8,128)(2,1)S(1)}, bf16[1,512,1536]{2,1,0:T(8,128)(2,1)}, u32[]{:S(2)}) copy-start(bf16[1,512,1536]{2,1,0:T(8,128)(2,1)} %param.6) | copy-start | bytes 4718596
  210.4 87.6 %all-to-all-start.1 = ((bf16[64,2,8,1536]{3,2,1,0:T(8,128)(2,1)}), bf16[64,2,8,1536]{3,2,1,0:T(8,128)(2,1)S(1)}, u32[]{:S(2)}, u32[]{:S(2)}) async-start(bf16[64,2,8,1536]{3,2,1,0:T(8,128)(2,1)} %select_select_fusion), calls=%async_computation.1 | async-start | bytes 6291456 | tf_op jit(solution)/shard_map/all_to_all | solution.py:81
Sparse Core Ops, SparseCore 0:
  16.5 179.2 reduce-scatter.3
  198.2 47.5 all-reduce.3
  248.8 85.4 all-gather.1
